TPU v7x, 32 devices: a whole 2x2x4 slice. The times are simulated.
32 devices in a mesh: dp: 4 (over z), seq: 8 (over y, x, core).
Axes of the slice: x: 2, y: 2, z: 4, core: 2. Of those that a mesh axis runs over, the one named last changes fastest.
Arguments:
- signal: bfloat16 [8, 1024, 1536], P('dp', 'seq'), may hold values from -6 to 6
- dilated_tap_weight: bfloat16 [3, 1536, 768], P(None, 'dp'), may hold values from -0.09375 to 0.09375
- out_weight: bfloat16 [768, 1536], P(None, 'dp'), may hold values from -0.21875 to 0.21875
- cotangent: bfloat16 [8, 1024, 1536], P('dp', 'seq'), may hold values from -6 to 6
Outputs:
- result: bfloat16 [8, 1024, 1536], P('dp', 'seq')
- grad_signal: bfloat16 [8, 1024, 1536], P('dp', 'seq')
All inputs are finite; a program needn't handle non-finite values.
Results may differ from a plain program's by a relative error of at most 0.0034.
Values may be sent and summed in bfloat16 or wider, within the bound.
No kernel may reach another device: no remote copies, remote signals or barrier semaphores. Data moves between devices by JAX's collectives and lax.ppermute only.
A program may use at most 64 MiB of HBM per device.

v0:
```python
import jax
import jax.numpy as jnp
from jax import lax
from jax.sharding import PartitionSpec as P

DILATION_STEP = 32


def extended(block, sides, width):
    for axis, dim in sides:
        count = lax.axis_size(axis)
        forward = [(i, i + 1) for i in range(count - 1)]
        backward = [(target, source) for source, target in forward]
        low = lax.ppermute(
            lax.slice_in_dim(block, block.shape[dim] - width, None, axis=dim), axis, forward
        )
        high = lax.ppermute(lax.slice_in_dim(block, 0, width, axis=dim), axis, backward)
        block = jnp.concatenate([low, block, high], axis=dim)
    return block


def gelu_pull(point, grad):
    _, pull = jax.vjp(jax.nn.gelu, point)
    return pull(grad)[0]


def forward_taps(gelu_output, padded_signal, convolution_filter):
    sequence_length = gelu_output.shape[1]
    preactivation = jnp.einsum(
        "xzi,iv->xzv",
        padded_signal[:, 0:sequence_length],
        convolution_filter[0],
        preferred_element_type=jnp.float32,
    )
    preactivation = preactivation + jnp.einsum(
        "xzi,iv->xzv",
        padded_signal[:, DILATION_STEP : DILATION_STEP + sequence_length],
        convolution_filter[1],
        preferred_element_type=jnp.float32,
    )
    preactivation = preactivation + jnp.einsum(
        "xzi,iv->xzv",
        padded_signal[:, 2 * DILATION_STEP : 2 * DILATION_STEP + sequence_length],
        convolution_filter[2],
        preferred_element_type=jnp.float32,
    )
    return preactivation


def backward_taps(gradient_preactivation, gradient_padded_input, convolution_filter):
    sequence_length = gradient_preactivation.shape[1]
    gradient_activation = jnp.einsum(
        "wth,ch->wtc",
        gradient_padded_input[:, 2 * DILATION_STEP : 2 * DILATION_STEP + sequence_length],
        convolution_filter[0],
        preferred_element_type=jnp.float32,
    )
    gradient_activation = gradient_activation + jnp.einsum(
        "wth,ch->wtc",
        gradient_padded_input[:, DILATION_STEP : DILATION_STEP + sequence_length],
        convolution_filter[1],
        preferred_element_type=jnp.float32,
    )
    gradient_activation = gradient_activation + jnp.einsum(
        "wth,ch->wtc",
        gradient_padded_input[:, 0:sequence_length],
        convolution_filter[2],
        preferred_element_type=jnp.float32,
    )
    return gradient_activation


def per_device(signal, dilated_tap_weight, out_weight, cotangent):
    convolution_filter, output_map = (
        lax.all_gather(dilated_tap_weight, "dp", axis=1, tiled=True),
        lax.all_gather(out_weight, "dp", axis=1, tiled=True),
    )
    signal_wide = signal.astype(jnp.float32)
    gelu_output = jax.nn.gelu(signal_wide).astype(jnp.bfloat16)
    padded_signal = extended(gelu_output, (("seq", 1),), DILATION_STEP)
    preactivation = forward_taps(gelu_output, padded_signal, convolution_filter)
    active = jax.nn.gelu(preactivation).astype(jnp.bfloat16)
    output = signal_wide + jnp.einsum(
        "wth,hc->wtc", active, output_map, preferred_element_type=jnp.float32
    )
    grad_active = jnp.einsum(
        "wtc,hc->wth", cotangent, output_map, preferred_element_type=jnp.float32
    )
    gradient_preactivation = gelu_pull(preactivation, grad_active).astype(jnp.bfloat16)
    gradient_padded_input = extended(gradient_preactivation, (("seq", 1),), DILATION_STEP)
    gradient_activation = backward_taps(
        gradient_preactivation, gradient_padded_input, convolution_filter
    )
    grad_in = cotangent.astype(jnp.float32) + gelu_pull(signal_wide, gradient_activation)
    return (output.astype(jnp.bfloat16), grad_in.astype(jnp.bfloat16))


def solution(mesh):
    return jax.shard_map(
        per_device,
        mesh=mesh,
        in_specs=(P("dp", "seq", None), P(None, "dp", None), P(None, "dp"), P("dp", "seq", None)),
        out_specs=(P("dp", "seq", None), P("dp", "seq", None)),
        check_vma=False,
    )
```

profile of v0, /device:TPU:1, one launch (start us, length us, event | category | flops | bytes accessed | tf_op | source)
XLA Modules:
  0.0 213.3 jit_solution(15958082162178033405)
XLA Ops:
  7.2 0.0 copy-start
  7.2 0.0 all-gather.3.cloned.1.call-start
  7.2 0.7 all-gather.3.cloned.1.call-update
  7.9 0.0 all-gather.5.cloned.1.call-start
  8.0 0.7 all-gather.5.cloned.1.call-update
  8.7 0.0 copy-done
  8.7 0.5 fusion.18
  9.2 4.5 %collective-permute-start = (bf16[2,32,1536]{2,1,0:T(8,128)(2,1)S(1)}, bf16[2,32,1536]{2,1,0:T(8,128)(2,1)S(1)}, u32[]{:S(2)}, u32[]{:S(2)}) collective-permute-start(bf16[2,32,1536]{2,1,0:T(8,128)(2,1)S(1)} %get-tuple-element.2), channel_id=1, source_target_pairs={{0,1},{1,2},{2,3},{3,4},{4,5},{5,6},{6,7},{8,9},{9,10},{10,11},{11... | collective-permute-start | bytes 589832 | tf_op jit(solution)/shard_map/ppermute | solution.py:14
  13.8 1.9 collective-permute-start.1
  15.7 124.4 %all-gather.3.cloned.1.call-done = bf16[3,1536,768]{2,1,0:T(8,128)(2,1)} async-done(((bf16[3,384,768]{2,1,0:T(8,128)(2,1)}), bf16[3,1536,768]{2,1,0:T(8,128)(2,1)}) %all-gather.3.cloned.1.call-update) | async-done | bytes 7077904 | tf_op jit(solution)/shard_map/all_gather | solution.py:75
  140.1 0.0 copy-start.1
  140.1 2.9 %fusion.8 = f32[2,128,768]{2,1,0:T(8,128)S(1)} fusion(bf16[3,1536,768]{2,1,0:T(8,128)(2,1)} %all-gather.3.cloned.1.call-done, bf16[2,128,1536]{2,1,0:T(8,128)(2,1)S(1)} %copy-done), kind=kOutput, calls=%fused_computation.18 | convolution fusion | flops 607911936 | bytes 3932160 | tf_op jit(solution)/shard_map/xzi,iv->xzv/dot_general | solution.py:35
  143.0 0.0 collective-permute-done.1
  143.0 0.8 copy-done.1
  143.8 0.8 fusion.10
  144.6 0.0 copy-start.3
  144.6 0.0 collective-permute-done
  144.6 0.8 fusion.22
  145.4 44.6 %all-gather.5.cloned.1.call-done = bf16[768,1536]{1,0:T(8,128)(2,1)} async-done(((bf16[768,384]{1,0:T(8,128)(2,1)}), bf16[768,1536]{1,0:T(8,128)(2,1)}) %all-gather.5.cloned.1.call-update) | async-done | bytes 2359312 | tf_op jit(solution)/shard_map/all_gather | solution.py:76
  190.0 0.0 copy-done.3
  190.0 0.0 copy-start.2
  190.0 0.0 slice-start
  190.0 2.9 %fusion.29 = bf16[2,128,768]{2,1,0:T(8,128)(2,1)S(1)} fusion(f32[2,128,768]{2,1,0:T(8,128)S(1)} %fusion.22, bf16[2,128,1536]{2,1,0:T(8,128)(2,1)S(1)} %copy-done.3, bf16[768,1536]{1,0:T(8,128)(2,1)} %all-gather.5.cloned.1.call-done), kind=kOutput, calls=%fused_computation.41 | convolution fusion | flops 607911936 | bytes 4325376 | tf_op jit(solution)/shard_map/wtc,hc->wth/dot_general | solution.py:86
  192.9 2.6 %collective-permute-start.2 = (bf16[2,32,768]{2,1,0:T(8,128)(2,1)S(1)}, bf16[2,32,768]{2,1,0:T(8,128)(2,1)S(1)}, u32[]{:S(2)}, u32[]{:S(2)}) collective-permute-start(bf16[2,32,768]{2,1,0:T(8,128)(2,1)S(1)} %get-tuple-element.4), channel_id=1, source_target_pairs={{1,0},{2,1},{3,2},{4,3},{5,4},{6,5},{7,6},{9,8},{10,9},{11,10},{12... | collective-permute-start | bytes 294920 | tf_op jit(solution)/shard_map/ppermute | solution.py:17
  195.5 0.0 slice-start.1
  195.5 3.3 %collective-permute-start.3 = (bf16[2,32,768]{2,1,0:T(8,128)(2,1)S(1)}, bf16[2,32,768]{2,1,0:T(8,128)(2,1)S(1)}, u32[]{:S(2)}, u32[]{:S(2)}) collective-permute-start(bf16[2,32,768]{2,1,0:T(8,128)(2,1)S(1)} %get-tuple-element.5), channel_id=1, source_target_pairs={{0,1},{1,2},{2,3},{3,4},{4,5},{5,6},{6,7},{8,9},{9,10},{10,11},{11... | collective-permute-start | bytes 294920 | tf_op jit(solution)/shard_map/ppermute | solution.py:14
  198.8 0.0 copy-done.2
  198.8 1.7 fusion.1
  200.5 2.5 %fusion.7 = f32[2,128,1536]{2,1,0:T(8,128)S(1)} fusion(bf16[2,128,768]{2,1,0:T(8,128)(2,1)S(1)} %fusion.29, bf16[3,1536,768]{2,1,0:T(8,128)(2,1)} %all-gather.3.cloned.1.call-done), kind=kOutput, calls=%fused_computation.17 | convolution fusion | flops 603979776 | bytes 4325376 | tf_op jit(solution)/shard_map/wth,ch->wtc/dot_general | solution.py:58
  203.0 0.0 collective-permute-done.3
  203.0 0.0 slice-done
  203.0 0.0 slice-done.1
  203.0 0.8 fusion.9
  203.8 0.0 collective-permute-done.2
  203.9 2.6 %fusion.14 = bf16[2,128,1536]{2,1,0:T(8,128)(2,1)} fusion(bf16[2,128,1536]{2,1,0:T(8,128)(2,1)S(1)} %copy-done, f32[2,128,1536]{2,1,0:T(8,128)S(1)} %fusion.9, f32[2,128,1536]{2,1,0:T(8,128)S(1)} %fusion.7, bf16[3,1536,768]{2,1,0:T(8,128)(2,1)S(1)} %bitcast.31, bf16[2,128,1536]{2,1,0:T(8,128)(2,1)S(1)} %copy-done.3, ...), kind=kOutput, calls=%fused_computation.24 | convolution fusion | flops 614596608 | bytes 8355840 | tf_op jit(solution)/shard_map/wth,ch->wtc/dot_general | solution.py:52
  (3 shorter events, 0.0 us)
Async XLA Ops:
  7.2 1.5 copy-start
  7.2 132.9 %all-gather.3.cloned.1.call-start = ((), (), s32[]{:S(2)}) async-start(), calls=%async_computation | async-start | bytes 8847360 | tf_op jit(solution)/shard_map/all_gather | solution.py:75
  7.9 182.1 %all-gather.5.cloned.1.call-start = ((), (), s32[]{:S(2)}) async-start(), calls=%async_computation.1 | async-start | bytes 2949120 | tf_op jit(solution)/shard_map/all_gather | solution.py:76
  9.2 135.4 %collective-permute-start = (bf16[2,32,1536]{2,1,0:T(8,128)(2,1)S(1)}, bf16[2,32,1536]{2,1,0:T(8,128)(2,1)S(1)}, u32[]{:S(2)}, u32[]{:S(2)}) collective-permute-start(bf16[2,32,1536]{2,1,0:T(8,128)(2,1)S(1)} %get-tuple-element.2), channel_id=1, source_target_pairs={{0,1},{1,2},{2,3},{3,4},{4,5},{5,6},{6,7},{8,9},{9,10},{10,11},{11... | collective-permute-start | bytes 589832 | tf_op jit(solution)/shard_map/ppermute | solution.py:14
  13.8 129.3 %collective-permute-start.1 = (bf16[2,32,1536]{2,1,0:T(8,128)(2,1)S(1)}, bf16[2,32,1536]{2,1,0:T(8,128)(2,1)S(1)}, u32[]{:S(2)}, u32[]{:S(2)}) collective-permute-start(bf16[2,32,1536]{2,1,0:T(8,128)(2,1)S(1)} %get-tuple-element.3), channel_id=1, source_target_pairs={{1,0},{2,1},{3,2},{4,3},{5,4},{6,5},{7,6},{9,8},{10,9},{11,10},{12... | collective-permute-start | bytes 589832 | tf_op jit(solution)/shard_map/ppermute | solution.py:17
  140.1 3.7 %copy-start.1 = (bf16[3,1536,768]{2,1,0:T(8,128)(2,1)S(1)}, bf16[3,1536,768]{2,1,0:T(8,128)(2,1)}, u32[]{:S(2)}) copy-start(bf16[3,1536,768]{2,1,0:T(8,128)(2,1)} %all-gather.3.cloned.1.call-done) | copy-start | bytes 21233668
  144.6 45.4 %copy-start.3 = (bf16[2,128,1536]{2,1,0:T(8,128)(2,1)S(1)}, bf16[2,128,1536]{2,1,0:T(8,128)(2,1)}, u32[]{:S(2)}) copy-start(bf16[2,128,1536]{2,1,0:T(8,128)(2,1)} %param.7) | copy-start | bytes 2359300
  190.0 8.8 %copy-start.2 = (bf16[768,1536]{1,0:T(8,128)(2,1)S(1)}, bf16[768,1536]{1,0:T(8,128)(2,1)}, u32[]{:S(2)}) copy-start(bf16[768,1536]{1,0:T(8,128)(2,1)} %all-gather.5.cloned.1.call-done) | copy-start | bytes 7077892
  190.0 13.0 %slice-start = ((s8[7077888]{0:T(1024)(128)(4,1)}), s8[4194304]{0:T(1024)(128)(4,1)S(1)}, s32[]{:S(2)}) async-start(s8[7077888]{0:T(1024)(128)(4,1)} %bitcast.30), calls=%async_computation.2 | async-start | bytes 8388608
  192.9 11.0 %collective-permute-start.2 = (bf16[2,32,768]{2,1,0:T(8,128)(2,1)S(1)}, bf16[2,32,768]{2,1,0:T(8,128)(2,1)S(1)}, u32[]{:S(2)}, u32[]{:S(2)}) collective-permute-start(bf16[2,32,768]{2,1,0:T(8,128)(2,1)S(1)} %get-tuple-element.4), channel_id=1, source_target_pairs={{1,0},{2,1},{3,2},{4,3},{5,4},{6,5},{7,6},{9,8},{10,9},{11,10},{12... | collective-permute-start | bytes 294920 | tf_op jit(solution)/shard_map/ppermute | solution.py:17
  195.5 7.5 %slice-start.1 = ((s8[7077888]{0:T(1024)(128)(4,1)}), s8[2883584]{0:T(1024)(128)(4,1)S(1)}, s32[]{:S(2)}) async-start(s8[7077888]{0:T(1024)(128)(4,1)} %bitcast.30), calls=%async_computation.3 | async-start | bytes 5767168
  195.5 7.5 %collective-permute-start.3 = (bf16[2,32,768]{2,1,0:T(8,128)(2,1)S(1)}, bf16[2,32,768]{2,1,0:T(8,128)(2,1)S(1)}, u32[]{:S(2)}, u32[]{:S(2)}) collective-permute-start(bf16[2,32,768]{2,1,0:T(8,128)(2,1)S(1)} %get-tuple-element.5), channel_id=1, source_target_pairs={{0,1},{1,2},{2,3},{3,4},{4,5},{5,6},{6,7},{8,9},{9,10},{10,11},{11... | collective-permute-start | bytes 294920 | tf_op jit(solution)/shard_map/ppermute | solution.py:14
Sparse Core Ops, SparseCore 0:
  9.6 130.4 all-gather.2
  141.7 48.2 all-gather.4
where the time goes:
time: 214 us; the launch traced here: 213 us
  waiting for transfers between devices  170 us (79%)
  matrix products  14.9 us (7%)
  between operations  14.2 us (7%)
  starting transfers between devices  12.4 us (6%)
    all_gather x1, waiting for transfers between devices, per_device(): lax.all_gather(dilated_tap_weight, 'dp', axis=1, tiled=True)  124 us
    all_gather x1, waiting for transfers between devices, per_device(): lax.all_gather(out_weight, 'dp', axis=1, tiled=True)  44.6 us
    ppermute x2, starting transfers between devices, extended(): lax.ppermute(lax.slice_in_dim(block, block.shape[dim] - width, None, axis...  7.76 us
    ppermute x2, starting transfers between devices, extended(): lax.ppermute(lax.slice_in_dim(block, 0, width, axis=dim), axis, backward)  4.54 us
  transfers between devices with their start and end apart: 6, of which 2 were waited for; matrix products, arithmetic and copies ran while one was open for 5% of the time, Pallas kernels for 0%

commit v1 on v0

--- a/solution.py
+++ b/solution.py
@@ -4,6 +4,28 @@
 from jax.sharding import PartitionSpec as P
 
 DILATION_STEP = 32
+
+
+def laid_out(blocks, dim):
+    blocks = jnp.moveaxis(blocks, 0, dim)
+    dims = blocks.shape
+    return blocks.reshape(*dims[:dim], dims[dim] * dims[dim + 1], *dims[dim + 2 :])
+
+
+def collect(x, axis, dim):
+    devices = lax.axis_size(axis)
+    pairs = [(i, (i + 1) % devices) for i in range(devices)]
+    back = [(b, a) for a, b in pairs]
+    lower, upper = ([], [])
+    for lap in range(devices - 1):
+        if lap % 2 == 0:
+            lower.append(lax.ppermute(lower[-1] if lower else x, axis, pairs))
+        else:
+            upper.append(lax.ppermute(upper[-1] if upper else x, axis, back))
+    blocks = jnp.stack([*lower[::-1], x, *upper])
+    shift = lax.axis_index(axis) - len(lower)
+    blocks = blocks[(jnp.arange(devices) - shift) % devices]
+    return laid_out(blocks, dim)
 
 
 def extended(block, sides, width):
@@ -73,7 +95,7 @@
 def per_device(signal, dilated_tap_weight, out_weight, cotangent):
     convolution_filter, output_map = (
         lax.all_gather(dilated_tap_weight, "dp", axis=1, tiled=True),
-        lax.all_gather(out_weight, "dp", axis=1, tiled=True),
+        collect(out_weight, "dp", 1),
     )
     signal_wide = signal.astype(jnp.float32)
     gelu_output = jax.nn.gelu(signal_wide).astype(jnp.bfloat16)

time: 214 us -> 196 us (0.916)
  waiting for transfers between devices: 170 us -> 128 us
  starting transfers between devices: 12.4 us -> 27.8 us
  local copies, waits for them, and re-layouts: 0.86 us -> 7.9 us
    all_gather x1 -> x0, waiting for transfers between devices: 44.6 us -> none  [per_device(): lax.all_gather(out_weight, 'dp', axis=1, tiled=True)]
    ppermute x0 -> x3, waiting for transfers between devices: none -> 44 us  [the longest x1 23.3 us: collect(): upper.append(lax.ppermute(upper[-1] if upper else x, axis, back))]
    all_gather x1, waiting for transfers between devices: 124 us -> 82.2 us  [per_device(): lax.all_gather(dilated_tap_weight, 'dp', axis=1, tiled=True)]
    ppermute x2, starting transfers between devices: 7.76 us -> 19.3 us  [extended(): lax.ppermute(lax.slice_in_dim(block, block.shape[dim] - width, None, axis...]
    ppermute x0 -> x3, starting transfers between devices: none -> 4.16 us  [the longest x2 2.13 us: collect(): lower.append(lax.ppermute(lower[-1] if lower else x, axis, pairs))]
    transpose x0 -> x1, local copies, waits for them, and re-layouts: none -> 2.85 us  [laid_out(): blocks = jnp.moveaxis(blocks, 0, dim)]
    gather x0 -> x1, local copies, waits for them, and re-layouts: none -> 2.36 us  [collect(): blocks = blocks[(jnp.arange(devices) - shift) % devices]]
  transfers between devices with their start and end apart: 6 -> 8, of which waited for: 2 -> 5; matrix products, arithmetic and copies ran while one was open for 5% -> 8% of each run, Pallas kernels for 0% -> 0%
where the time goes in v1:
time: 196 us; the launch traced here: 194 us
  waiting for transfers between devices  128 us (65%)
  starting transfers between devices  27.8 us (14%)
  between operations  14.2 us (7%)
  matrix products  13.8 us (7%)
  local copies, waits for them, and re-layouts  7.9 us (4%)
  other arithmetic  2.53 us (1%)
    all_gather x1, waiting for transfers between devices, per_device(): lax.all_gather(dilated_tap_weight, 'dp', axis=1, tiled=True)  82.2 us
    ppermute x1, waiting for transfers between devices, collect(): upper.append(lax.ppermute(upper[-1] if upper else x, axis, back))  23.3 us
    ppermute x2, waiting for transfers between devices, collect(): lower.append(lax.ppermute(lower[-1] if lower else x, axis, pairs))  20.7 us
    ppermute x2, starting transfers between devices, extended(): lax.ppermute(lax.slice_in_dim(block, block.shape[dim] - width, None, axis...  19.3 us
    ppermute x2, starting transfers between devices, extended(): lax.ppermute(lax.slice_in_dim(block, 0, width, axis=dim), axis, backward)  4.28 us
  transfers between devices with their start and end apart: 8, of which 5 were waited for; matrix products, arithmetic and copies ran while one was open for 8% of the time, Pallas kernels for 0%

profile of v1, /device:TPU:1, one launch (start us, length us, event | category | flops | bytes accessed | tf_op | source)
XLA Modules:
  0.0 193.9 jit_solution(14885305589910751036)
XLA Ops:
  7.2 0.0 copy-start.2
  7.2 0.0 copy-start
  7.2 0.0 all-gather.2.cloned.1.call-start
  7.2 0.7 all-gather.2.cloned.1.call-update
  7.9 0.3 copy-done.2
  8.2 2.1 %collective-permute-start.2 = (bf16[768,384]{1,0:T(8,128)(2,1)S(1)}, bf16[768,384]{1,0:T(8,128)(2,1)S(1)}, u32[]{:S(2)}, u32[]{:S(2)}) collective-permute-start(bf16[768,384]{1,0:T(8,128)(2,1)S(1)} %copy-done.2), channel_id=1, source_target_pairs={{0,8},{8,16},{16,24},{24,0},{1,9},{9,17},{17,25},{25,1},{2,10},{10... | collective-permute-start | bytes 1769480 | tf_op jit(solution)/shard_map/ppermute | solution.py:22
  10.4 2.0 %collective-permute-start.4 = (bf16[768,384]{1,0:T(8,128)(2,1)S(1)}, bf16[768,384]{1,0:T(8,128)(2,1)S(1)}, u32[]{:S(2)}, u32[]{:S(2)}) collective-permute-start(bf16[768,384]{1,0:T(8,128)(2,1)S(1)} %copy-done.2), channel_id=1, source_target_pairs={{8,0},{16,8},{24,16},{0,24},{9,1},{17,9},{25,17},{1,25},{10,2},{18... | collective-permute-start | bytes 1769480 | tf_op jit(solution)/shard_map/ppermute | solution.py:24
  12.4 0.0 copy-done
  12.4 0.5 fusion.15
  12.9 12.5 %collective-permute-done.2 = bf16[768,384]{1,0:T(8,128)(2,1)S(1)} collective-permute-done((bf16[768,384]{1,0:T(8,128)(2,1)S(1)}, bf16[768,384]{1,0:T(8,128)(2,1)S(1)}, u32[]{:S(2)}, u32[]{:S(2)}) %collective-permute-start.2) | collective-permute-done | bytes 589856 | tf_op jit(solution)/shard_map/ppermute | solution.py:22
  25.5 0.0 copy-start.3
  25.5 0.0 collective-permute-start.3
  25.5 0.8 fusion.46
  26.2 16.1 %collective-permute-start = (bf16[2,32,1536]{2,1,0:T(8,128)(2,1)S(1)}, bf16[2,32,1536]{2,1,0:T(8,128)(2,1)}, u32[]{:S(2)}, u32[]{:S(2)}) collective-permute-start(bf16[2,32,1536]{2,1,0:T(8,128)(2,1)S(1)} %get-tuple-element.2), channel_id=1, source_target_pairs={{0,1},{1,2},{2,3},{3,4},{4,5},{5,6},{6,7},{8,9},{9,10},{10,11},{11... | collective-permute-start | bytes 589832 | tf_op jit(solution)/shard_map/ppermute | solution.py:36
  42.3 1.9 collective-permute-start.1
  44.3 23.3 %collective-permute-done.4 = bf16[768,384]{1,0:T(8,128)(2,1)S(1)} collective-permute-done((bf16[768,384]{1,0:T(8,128)(2,1)S(1)}, bf16[768,384]{1,0:T(8,128)(2,1)S(1)}, u32[]{:S(2)}, u32[]{:S(2)}) %collective-permute-start.4) | collective-permute-done | bytes 589856 | tf_op jit(solution)/shard_map/ppermute | solution.py:24
  67.6 0.0 copy-start.4
  67.6 8.2 %collective-permute-done.3 = bf16[768,384]{1,0:T(8,128)(2,1)S(1)} collective-permute-done((bf16[768,384]{1,0:T(8,128)(2,1)S(1)}, bf16[768,384]{1,0:T(8,128)(2,1)S(1)}, u32[]{:S(2)}, u32[]{:S(2)}) %collective-permute-start.3) | collective-permute-done | bytes 589856 | tf_op jit(solution)/shard_map/ppermute | solution.py:22
  75.8 0.0 copy-start.5
  75.8 0.0 copy-done.3
  75.8 0.0 copy-done.4
  75.8 0.8 copy-done.5
  76.6 2.0 %pad_maximum_fusion = bf16[4,768,384]{2,1,0:T(8,128)(2,1)S(1)} fusion(bf16[1,768,384]{2,1,0:T(8,128)(2,1)} %bitcast.45, bf16[1,768,384]{2,1,0:T(8,128)(2,1)} %bitcast.43, bf16[1,768,384]{2,1,0:T(8,128)(2,1)} %bitcast.44, bf16[1,768,384]{2,1,0:T(8,128)(2,1)} %bitcast.46), kind=kLoop, calls=%fused_computation.13 | loop fusion | flops 3538944 | bytes 4718592 | tf_op jit(solution)/shard_map/stack | solution.py:25
  78.5 2.4 %gather_fusion = bf16[4,768,384]{2,1,0:T(8,128)(2,1)} fusion(bf16[4,768,384]{2,1,0:T(8,128)(2,1)S(1)} %pad_maximum_fusion, s32[1024]{0:T(1024)S(1)} %pad_clamp_fusion), kind=kCustom, calls=%fused_computation | custom fusion | bytes 4718608 | tf_op jit(solution)/shard_map/gather | solution.py:27
  80.9 2.8 %copy.8 = bf16[768,4,384]{0,2,1:T(8,128)(2,1)S(1)} copy(bf16[768,4,384]{2,0,1:T(8,128)(2,1)} %bitcast.40) | data formatting | bytes 4718592 | tf_op jit(solution)/shard_map/transpose | solution.py:10
  83.8 82.2 %all-gather.2.cloned.1.call-done = bf16[3,1536,768]{2,1,0:T(8,128)(2,1)} async-done(((bf16[3,384,768]{2,1,0:T(8,128)(2,1)}), bf16[3,1536,768]{2,1,0:T(8,128)(2,1)}) %all-gather.2.cloned.1.call-update) | async-done | bytes 7077904 | tf_op jit(solution)/shard_map/all_gather | solution.py:97
  165.9 0.0 copy-start.6
  165.9 3.1 %fusion.5 = f32[2,128,768]{2,1,0:T(8,128)S(1)} fusion(bf16[3,1536,768]{2,1,0:T(8,128)(2,1)} %all-gather.2.cloned.1.call-done, bf16[2,128,1536]{2,1,0:T(8,128)(2,1)} %param.4), kind=kOutput, calls=%fused_computation.17 | convolution fusion | flops 607911936 | bytes 3932160 | tf_op jit(solution)/shard_map/xzi,iv->xzv/dot_general | solution.py:57
  169.1 0.0 collective-permute-done.1
  169.1 0.8 copy-done.6
  169.9 1.7 fusion.7
  171.6 0.0 copy-start.1
  171.6 0.0 collective-permute-done
  171.6 1.8 fusion.19
  173.4 0.0 copy-done.1
  173.4 0.0 copy-start.7
  173.4 1.8 fusion.1
  175.2 0.0 copy-done.7
  175.2 1.2 fusion.26
  176.4 2.4 %collective-permute-start.5 = (bf16[2,32,768]{2,1,0:T(8,128)(2,1)S(1)}, bf16[2,32,768]{2,1,0:T(8,128)(2,1)S(1)}, u32[]{:S(2)}, u32[]{:S(2)}) collective-permute-start(bf16[2,32,768]{2,1,0:T(8,128)(2,1)S(1)} %get-tuple-element.4), channel_id=1, source_target_pairs={{1,0},{2,1},{3,2},{4,3},{5,4},{6,5},{7,6},{9,8},{10,9},{11,10},{12... | collective-permute-start | bytes 294920 | tf_op jit(solution)/shard_map/ppermute | solution.py:39
  178.8 3.2 %collective-permute-start.6 = (bf16[2,32,768]{2,1,0:T(8,128)(2,1)S(1)}, bf16[2,32,768]{2,1,0:T(8,128)(2,1)S(1)}, u32[]{:S(2)}, u32[]{:S(2)}) collective-permute-start(bf16[2,32,768]{2,1,0:T(8,128)(2,1)S(1)} %get-tuple-element.5), channel_id=1, source_target_pairs={{0,1},{1,2},{2,3},{3,4},{4,5},{5,6},{6,7},{8,9},{9,10},{10,11},{11... | collective-permute-start | bytes 294920 | tf_op jit(solution)/shard_map/ppermute | solution.py:36
  182.0 0.8 fusion.4
  182.8 0.8 collective-permute-done.6
  183.6 0.8 fusion.6
  184.4 0.0 collective-permute-done.5
  184.4 2.6 %fusion.11 = bf16[2,128,1536]{2,1,0:T(8,128)(2,1)} fusion(bf16[2,128,1536]{2,1,0:T(8,128)(2,1)S(1)} %copy-done.1, f32[2,128,1536]{2,1,0:T(8,128)S(1)} %fusion.6, f32[2,128,1536]{2,1,0:T(8,128)S(1)} %fusion.4, bf16[3,1536,768]{2,1,0:T(8,128)(2,1)S(1)} %copy-done.6, bf16[2,128,1536]{2,1,0:T(8,128)(2,1)S(1)} %copy-done.7, ...), kind=kOutput, calls=%fused_computation.23 | convolution fusion | flops 614596608 | bytes 8355840 | tf_op jit(solution)/shard_map/wth,ch->wtc/dot_general | solution.py:74
  (3 shorter events, 0.0 us)
Async XLA Ops:
  7.2 1.1 copy-start.2
  7.2 5.2 %copy-start = (bf16[2,128,1536]{2,1,0:T(8,128)(2,1)S(1)}, bf16[2,128,1536]{2,1,0:T(8,128)(2,1)}, u32[]{:S(2)}) copy-start(bf16[2,128,1536]{2,1,0:T(8,128)(2,1)} %param.4) | copy-start | bytes 2359300
  7.2 158.8 %all-gather.2.cloned.1.call-start = ((), (), s32[]{:S(2)}) async-start(), calls=%async_computation | async-start | bytes 8847360 | tf_op jit(solution)/shard_map/all_gather | solution.py:97
  8.2 17.2 %collective-permute-start.2 = (bf16[768,384]{1,0:T(8,128)(2,1)S(1)}, bf16[768,384]{1,0:T(8,128)(2,1)S(1)}, u32[]{:S(2)}, u32[]{:S(2)}) collective-permute-start(bf16[768,384]{1,0:T(8,128)(2,1)S(1)} %copy-done.2), channel_id=1, source_target_pairs={{0,8},{8,16},{16,24},{24,0},{1,9},{9,17},{17,25},{25,1},{2,10},{10... | collective-permute-start | bytes 1769480 | tf_op jit(solution)/shard_map/ppermute | solution.py:22
  10.4 57.2 %collective-permute-start.4 = (bf16[768,384]{1,0:T(8,128)(2,1)S(1)}, bf16[768,384]{1,0:T(8,128)(2,1)S(1)}, u32[]{:S(2)}, u32[]{:S(2)}) collective-permute-start(bf16[768,384]{1,0:T(8,128)(2,1)S(1)} %copy-done.2), channel_id=1, source_target_pairs={{8,0},{16,8},{24,16},{0,24},{9,1},{17,9},{25,17},{1,25},{10,2},{18... | collective-permute-start | bytes 1769480 | tf_op jit(solution)/shard_map/ppermute | solution.py:24
  25.5 50.3 %copy-start.3 = (bf16[768,384]{1,0:T(8,128)(2,1)}, bf16[768,384]{1,0:T(8,128)(2,1)S(1)}, u32[]{:S(2)}) copy-start(bf16[768,384]{1,0:T(8,128)(2,1)S(1)} %collective-permute-done.2) | copy-start | bytes 1769476
  25.5 50.3 %collective-permute-start.3 = (bf16[768,384]{1,0:T(8,128)(2,1)S(1)}, bf16[768,384]{1,0:T(8,128)(2,1)S(1)}, u32[]{:S(2)}, u32[]{:S(2)}) collective-permute-start(bf16[768,384]{1,0:T(8,128)(2,1)S(1)} %collective-permute-done.2), channel_id=1, source_target_pairs={{0,8},{8,16},{16,24},{24,0},{1,9},{9,17},{17,25},{25,1},{2,10},{10... | collective-permute-start | bytes 1769480 | tf_op jit(solution)/shard_map/ppermute | solution.py:22
  26.2 145.4 %collective-permute-start = (bf16[2,32,1536]{2,1,0:T(8,128)(2,1)S(1)}, bf16[2,32,1536]{2,1,0:T(8,128)(2,1)}, u32[]{:S(2)}, u32[]{:S(2)}) collective-permute-start(bf16[2,32,1536]{2,1,0:T(8,128)(2,1)S(1)} %get-tuple-element.2), channel_id=1, source_target_pairs={{0,1},{1,2},{2,3},{3,4},{4,5},{5,6},{6,7},{8,9},{9,10},{10,11},{11... | collective-permute-start | bytes 589832 | tf_op jit(solution)/shard_map/ppermute | solution.py:36
  42.3 126.8 %collective-permute-start.1 = (bf16[2,32,1536]{2,1,0:T(8,128)(2,1)}, bf16[2,32,1536]{2,1,0:T(8,128)(2,1)}, u32[]{:S(2)}, u32[]{:S(2)}) collective-permute-start(bf16[2,32,1536]{2,1,0:T(8,128)(2,1)} %get-tuple-element.3), channel_id=1, source_target_pairs={{1,0},{2,1},{3,2},{4,3},{5,4},{6,5},{7,6},{9,8},{10,9},{11,10},{12... | collective-permute-start | bytes 589832 | tf_op jit(solution)/shard_map/ppermute | solution.py:39
  67.6 8.2 %copy-start.4 = (bf16[768,384]{1,0:T(8,128)(2,1)}, bf16[768,384]{1,0:T(8,128)(2,1)S(1)}, u32[]{:S(2)}) copy-start(bf16[768,384]{1,0:T(8,128)(2,1)S(1)} %collective-permute-done.4) | copy-start | bytes 1769476
  75.8 0.8 copy-start.5
  165.9 4.0 %copy-start.6 = (bf16[3,1536,768]{2,1,0:T(8,128)(2,1)S(1)}, bf16[3,1536,768]{2,1,0:T(8,128)(2,1)}, u32[]{:S(2)}) copy-start(bf16[3,1536,768]{2,1,0:T(8,128)(2,1)} %all-gather.2.cloned.1.call-done) | copy-start | bytes 21233668
  171.6 1.8 copy-start.1
  173.4 1.8 copy-start.7
  176.4 8.0 %collective-permute-start.5 = (bf16[2,32,768]{2,1,0:T(8,128)(2,1)S(1)}, bf16[2,32,768]{2,1,0:T(8,128)(2,1)S(1)}, u32[]{:S(2)}, u32[]{:S(2)}) collective-permute-start(bf16[2,32,768]{2,1,0:T(8,128)(2,1)S(1)} %get-tuple-element.4), channel_id=1, source_target_pairs={{1,0},{2,1},{3,2},{4,3},{5,4},{6,5},{7,6},{9,8},{10,9},{11,10},{12... | collective-permute-start | bytes 294920 | tf_op jit(solution)/shard_map/ppermute | solution.py:39
  178.8 4.8 %collective-permute-start.6 = (bf16[2,32,768]{2,1,0:T(8,128)(2,1)S(1)}, bf16[2,32,768]{2,1,0:T(8,128)(2,1)S(1)}, u32[]{:S(2)}, u32[]{:S(2)}) collective-permute-start(bf16[2,32,768]{2,1,0:T(8,128)(2,1)S(1)} %get-tuple-element.5), channel_id=1, source_target_pairs={{0,1},{1,2},{2,3},{3,4},{4,5},{5,6},{6,7},{8,9},{9,10},{10,11},{11... | collective-permute-start | bytes 294920 | tf_op jit(solution)/shard_map/ppermute | solution.py:36
Sparse Core Ops, SparseCore 0:
  9.6 156.3 all-gather.1
